TPU v7x, 32 devices: a whole 2x2x4 slice. The times are simulated.
32 devices in a mesh: dp: 16 (over z, y, core), tensor: 2 (over x).
Axes of the slice: x: 2, y: 2, z: 4, core: 2. Of those that a mesh axis runs over, the one named last changes fastest.
Arguments:
- clip_feats: bfloat16 [2048, 1280], P('dp', 'tensor'), may hold values from -3 to 3
- proj_weight: bfloat16 [1280, 512], P('tensor'), may hold values from -1 to 1
- caption_emb: bfloat16 [2048, 512], P(('dp', 'tensor')), may hold values from -1.25 to 1.25
- logit_scale: float32 [1], replicated, may hold values from 20 to 400
- pair_perm: int32 [2048], replicated, may hold values from 0 to 2047, as said below
Outputs:
- clip_grad: float32 [2048, 1280], P('dp', 'tensor')
- caption_grad: float32 [2048, 512], P(('dp', 'tensor'))
- row_loss: float32 [2048], P('dp')
Inputs may be any that keep to these rules, and one draw needn't show every extreme that they name: pair_perm is a permutation of the 2048 caption indices.
All inputs are finite; a program needn't handle non-finite values.
Results may differ from a plain program's by a relative error of at most 0.012.
The roundings to bfloat16 on the way count: a program that leaves them out, or rounds other values in their place, can miss the bound.
Values may be sent and summed in bfloat16 or wider, within the bound.
A program may use at most 64 MiB of HBM per device.

v0:
```python
import jax
import jax.numpy as jnp
from jax import lax
from jax.sharding import PartitionSpec as P

norm_eps = 1e-06


def unit_rows(values):
    squares = jnp.sum(values * values, axis=1, keepdims=True)
    inverse = lax.rsqrt(squares + norm_eps)
    return (values * inverse, inverse)


def score_slab(videos, slab_rows, offset, target, logit):
    scores = logit * lax.dot_general(
        videos, slab_rows, (((1,), (1,)), ((), ())), preferred_element_type=jnp.float32
    )
    column = offset + jnp.arange(slab_rows.shape[0], dtype=jnp.int32)
    onehot = (column[None, :] == target[:, None]).astype(jnp.float32)
    return (scores, onehot)


def fold_stats(carry, slab_rows, offset, videos, target, logit):
    run_max, run_sum, run_pos = carry
    scores, onehot = score_slab(videos, slab_rows, offset, target, logit)
    new_max = jnp.maximum(run_max, jnp.max(scores, axis=1))
    run_sum = jnp.sum(jnp.exp(scores - new_max[:, None]), axis=1)
    run_pos = jnp.sum(scores * onehot, axis=1)
    return (new_max, run_sum, run_pos)


def slab_weights(slab_rows, offset, videos, target, logit, row_max, row_sum):
    scores, onehot = score_slab(videos, slab_rows, offset, target, logit)
    weights = (jnp.exp(scores - row_max[:, None]) / row_sum[:, None] - onehot).astype(jnp.bfloat16)
    vid_part = logit * jnp.dot(weights, slab_rows, preferred_element_type=jnp.float32)
    return (weights, vid_part)


def body(clip_feats, proj_weight, caption_emb, logit_scale, pair_perm):
    logit = logit_scale[0]
    partial_value = jnp.dot(clip_feats, proj_weight, preferred_element_type=jnp.float32)
    raw_proj = lax.psum(partial_value, "tensor")
    unit_vid, vid_inv = unit_rows(raw_proj)
    videos = unit_vid.astype(jnp.bfloat16)
    cap_unit, cap_inv = unit_rows(caption_emb.astype(jnp.float32))
    captions = cap_unit.astype(jnp.bfloat16)
    row_count = videos.shape[0]
    cap_count = captions.shape[0]
    groups = lax.axis_size("tensor")
    tensor_pos = lax.axis_index("tensor")
    wanted = lax.dynamic_slice_in_dim(pair_perm, lax.axis_index("dp") * row_count, row_count, 0)
    owner_block = wanted // cap_count
    local_col = owner_block // groups * cap_count + wanted % cap_count
    target = jnp.where(owner_block % groups == tensor_pos, local_col, -1)
    start_stats = (
        jnp.full((row_count,), -1e30, jnp.float32),
        jnp.zeros((row_count,), jnp.float32),
        jnp.zeros((row_count,), jnp.float32),
    )
    gathered = lax.all_gather(captions, "dp", axis=0, tiled=True)
    stats = fold_stats(start_stats, gathered, 0, videos, target, logit)
    row_max = lax.pmax(stats[0], "tensor")
    row_sum, row_pos = lax.psum((stats[1] * jnp.exp(stats[0] - row_max), stats[2]), "tensor")
    losses = row_max + jnp.log(row_sum) - row_pos
    weights_all, vid_part = slab_weights(gathered, 0, videos, target, logit, row_max, row_sum)
    vid_grad = lax.psum(vid_part, "tensor")
    cap_part = logit * lax.dot_general(
        weights_all, videos, (((0,), (0,)), ((), ())), preferred_element_type=jnp.float32
    )
    cap_grad = lax.psum_scatter(cap_part, "dp", scatter_dimension=0, tiled=True)
    vid_dot = jnp.sum(unit_vid * vid_grad, axis=1, keepdims=True)
    raw_grad = ((vid_grad - unit_vid * vid_dot) * vid_inv).astype(jnp.bfloat16)
    clip_grad = lax.dot_general(
        raw_grad, proj_weight, (((1,), (1,)), ((), ())), preferred_element_type=jnp.float32
    )
    cap_dot = jnp.sum(cap_unit * cap_grad, axis=1, keepdims=True)
    caption_grad = (cap_grad - cap_unit * cap_dot) * cap_inv
    return (clip_grad, caption_grad, losses)


def solution(mesh):
    return jax.shard_map(
        body,
        mesh=mesh,
        in_specs=(P("dp", "tensor"), P("tensor", None), P(("dp", "tensor"), None), P(), P()),
        out_specs=(P("dp", "tensor"), P(("dp", "tensor"), None), P("dp")),
        check_vma=False,
    )
```

profile of v0, /device:TPU:0, one launch (start us, length us, event | category | flops | bytes accessed | tf_op | source)
XLA Modules:
  0.0 143.4 jit_solution(11747821214149107070)
XLA Ops:
  8.1 1.0 copy-done
  9.1 1.9 %fusion.12 = f32[128,512]{1,0:T(8,128)} fusion(bf16[128,640]{1,0:T(8,128)(2,1)} %param.5, bf16[640,512]{1,0:T(8,128)(2,1)S(1)} %copy-done), kind=kOutput, calls=%fused_computation.41 | convolution fusion | flops 83886080 | bytes 1081344 | tf_op jit(solution)/shard_map/dot_general | solution.py:42
  11.0 0.0 all-gather.2.cloned.1.call-start
  11.1 1.0 fusion.6
  12.0 1.6 %fusion.2 = bf16[64,512]{1,0:T(8,128)(2,1)} fusion(bf16[64,512]{1,0:T(8,128)(2,1)} %param.7, f32[64]{0:T(128)S(1)} %add_rsqrt_fusion), kind=kLoop, calls=%fused_computation.15 | loop fusion | flops 98304 | bytes 131328 | tf_op jit(solution)/shard_map/convert_element_type | solution.py:47
  13.6 0.0 all-reduce.6.cloned.1.call-start
  14.3 0.8 compare_select_fusion
  15.1 22.6 %all-reduce.4.cloned.1.call-done = f32[128,512]{1,0:T(8,128)} async-done(((f32[128,512]{1,0:T(8,128)}), f32[128,512]{1,0:T(8,128)}) %all-reduce.4.cloned.1.call-update) | async-done | bytes 262160 | tf_op jit(solution)/shard_map/psum | solution.py:43
  37.7 1.1 multiply_reduce_fusion.1
  38.8 16.0 %all-gather.2.cloned.1.call-done = bf16[1024,512]{1,0:T(8,128)(2,1)} async-done(((bf16[64,512]{1,0:T(8,128)(2,1)}), bf16[1024,512]{1,0:T(8,128)(2,1)}) %all-gather.2.cloned.1.call-update) | async-done | bytes 1048592 | tf_op jit(solution)/shard_map/all_gather | solution.py:61
  54.8 1.9 %fusion.11 = (f32[128]{0:T(128)S(1)}, f32[128,1024]{1,0:T(8,128)S(1)}) fusion(bf16[1024,512]{1,0:T(8,128)(2,1)} %all-gather.2.cloned.1.call-done, f32[128,512]{1,0:T(8,128)} %all-reduce.4.cloned.1.call-done, f32[128]{0:T(128)S(1)} %add_rsqrt_fusion.1, f32[]{:T(128)} %bitcast.7), kind=kOutput, calls=%fused_computation.40 | convolution fusion | flops 134610816 | bytes 1836036 | tf_op jit(solution)/shard_map/dot_general | solution.py:16
  56.8 5.1 %pmax.7 = f32[128]{0:T(128)S(1)} all-reduce(f32[128]{0:T(128)S(1)} %broadcast_maximum_fusion), channel_id=1, replica_groups=mesh['dp'=16,'tensor'=2] {'tensor'}, use_global_device_ids=true, to_apply=%region_4.5 | all-reduce | flops 128 | bytes 1024 | tf_op jit(solution)/shard_map/pmax | solution.py:63
  61.9 0.3 select_reduce_fusion
  62.2 4.9 %all-reduce = (f32[128]{0:T(128)S(1)}, f32[128]{0:T(128)S(1)}) all-reduce(f32[128]{0:T(128)S(1)} %exponential_multiply_fusion, f32[128]{0:T(128)S(1)} %get-tuple-element.3), channel_id=1, replica_groups=mesh['dp'=16,'tensor'=2] {'tensor'}, use_global_device_ids=true, to_apply=%region_6.7 | all-reduce | flops 256 | bytes 2048 | tf_op jit(solution)/shard_map/psum | solution.py:64
  67.1 1.1 convolution_multiply_fusion.2
  68.2 0.0 reduce-scatter.2.cloned.1.call-start
  68.3 2.0 %convolution_multiply_fusion = f32[1024,512]{1,0:T(8,128)} fusion(f32[]{:T(128)} %bitcast.8, f32[128,512]{1,0:T(8,128)S(1)} %copy-done.1, f32[128]{0:T(128)S(1)} %add_rsqrt_fusion.1, f32[128,1024]{1,0:T(8,128)S(1)} %get-tuple-element.8, s32[128]{0:T(128)S(1)} %compare_select_fusion, f32[128]{0:T(128)S(1)} %get-tuple-element.5, f32[128]{0:T(128)S(1)} %pmax.7), kind=kOutput, calls=%fused_computation | convolution fusion | flops 135659520 | bytes 2885636 | tf_op jit(solution)/shard_map/dot_general | solution.py:68
  70.3 0.5 add_subtract_fusion
  70.8 19.9 %all-reduce.6.cloned.1.call-done = f32[128,512]{1,0:T(8,128)} async-done(((f32[128,512]{1,0:T(8,128)}), f32[128,512]{1,0:T(8,128)}) %all-reduce.6.cloned.1.call-update) | async-done | bytes 262160 | tf_op jit(solution)/shard_map/psum | solution.py:67
  90.7 1.1 multiply_reduce_fusion
  91.8 2.0 %fusion.7 = f32[128,640]{1,0:T(8,128)} fusion(bf16[640,512]{1,0:T(8,128)(2,1)S(1)} %copy-done, f32[128,512]{1,0:T(8,128)} %all-reduce.6.cloned.1.call-done, f32[128,512]{1,0:T(8,128)S(1)} %copy-done.1, f32[128]{0:T(128)S(1)} %multiply_reduce_fusion, f32[128]{0:T(128)S(1)} %add_rsqrt_fusion.1), kind=kOutput, calls=%fused_computation.20 | convolution fusion | flops 84213760 | bytes 1508352 | tf_op jit(solution)/shard_map/dot_general | solution.py:74
  93.9 39.4 %reduce-scatter.2.cloned.1.call-done = f32[64,512]{1,0:T(8,128)} async-done(((f32[1024,512]{1,0:T(8,128)}), f32[64,512]{1,0:T(8,128)}) %reduce-scatter.2.cloned.1.call-update) | async-done | bytes 131088 | tf_op jit(solution)/shard_map/reduce_scatter | solution.py:71
  133.3 1.1 fusion.3
  134.3 1.7 %fusion.5 = f32[64,512]{1,0:T(8,128)} fusion(f32[64,512]{1,0:T(8,128)} %reduce-scatter.2.cloned.1.call-done, bf16[64,512]{1,0:T(8,128)(2,1)S(1)} %copy-done.2, f32[64]{0:T(128)S(1)} %fusion.3, f32[64]{0:T(128)S(1)} %add_rsqrt_fusion), kind=kLoop, calls=%fused_computation.18 | loop fusion | flops 163840 | bytes 328192 | tf_op jit(solution)/shard_map/mul | solution.py:78
  (16 shorter events, 0.1 us)
Async XLA Ops:
  8.0 1.1 copy-start
  8.0 29.7 %all-reduce.4.cloned.1.call-start = ((), (), s32[]{:S(2)}) async-start(), calls=%async_computation.1 | async-start | bytes 524288 | tf_op jit(solution)/shard_map/psum | solution.py:43
  11.0 43.8 %all-gather.2.cloned.1.call-start = ((), (), s32[]{:S(2)}) async-start(), calls=%async_computation.2 | async-start | bytes 1114112 | tf_op jit(solution)/shard_map/all_gather | solution.py:61
  13.6 77.1 %all-reduce.6.cloned.1.call-start = ((), (), s32[]{:S(2)}) async-start(), calls=%async_computation.3 | async-start | bytes 524288 | tf_op jit(solution)/shard_map/psum | solution.py:67
  54.8 12.3 %copy-start.3 = (bf16[1024,512]{1,0:T(8,128)(2,1)S(1)}, bf16[1024,512]{1,0:T(8,128)(2,1)}, u32[]{:S(2)}) copy-start(bf16[1024,512]{1,0:T(8,128)(2,1)} %all-gather.2.cloned.1.call-done) | copy-start | bytes 3145732
  56.8 11.5 %copy-start.1 = (f32[128,512]{1,0:T(8,128)S(1)}, f32[128,512]{1,0:T(8,128)}, u32[]{:S(2)}) copy-start(f32[128,512]{1,0:T(8,128)} %all-reduce.4.cloned.1.call-done) | copy-start | bytes 786436
  68.2 65.0 %reduce-scatter.2.cloned.1.call-start = ((), (), s32[]{:S(2)}) async-start(), calls=%async_computation.4 | async-start | bytes 2228224 | tf_op jit(solution)/shard_map/reduce_scatter | solution.py:71
  70.2 63.0 %copy-start.2 = (bf16[64,512]{1,0:T(8,128)(2,1)S(1)}, bf16[64,512]{1,0:T(8,128)(2,1)}, u32[]{:S(2)}) copy-start(bf16[64,512]{1,0:T(8,128)(2,1)} %param.7) | copy-start | bytes 196612
Sparse Core Ops, SparseCore 0:
  11.7 26.0 all-reduce.3
  68.3 22.3 all-reduce.5
Sparse Core Ops, SparseCore 1:
  14.2 40.6 all-gather.1
  72.4 60.8 reduce-scatter.1
where the time goes:
time: 144 us; the launch traced here: 143 us
  waiting for transfers between devices  98 us (68%)
  between operations  16.2 us (11%)
  blocking collectives  10 us (7%)
  other arithmetic  9.03 us (6%)
  matrix products  8.93 us (6%)
    reduce_scatter x1, waiting for transfers between devices, body(): cap_grad = lax.psum_scatter(cap_part, 'dp', scatter_dimension=0, tiled=True)  39.4 us
    psum x1, waiting for transfers between devices, body(): raw_proj = lax.psum(partial_value, 'tensor')  22.6 us
    psum x1, waiting for transfers between devices, body(): vid_grad = lax.psum(vid_part, 'tensor')  19.9 us
    all_gather x1, waiting for transfers between devices, body(): gathered = lax.all_gather(captions, 'dp', axis=0, tiled=True)  16 us
    pmax x1, blocking collectives, body(): row_max = lax.pmax(stats[0], 'tensor')  5.07 us
    psum x1, blocking collectives, body(): lax.psum((stats[1] * jnp.exp(stats[0] - row_max), stats[2]), 'tensor')  4.93 us
  transfers between devices with their start and end apart: 4, of which 4 were waited for; matrix products, arithmetic and copies ran while one was open for 7% of the time, Pallas kernels for 0%

commit v1 on v0

v1 whole, which is shorter than its diff:
```python
import functools

import jax
import jax.numpy as jnp
from jax import lax
from jax.experimental import pallas as pl
from jax.experimental.pallas import tpu as pltpu
from jax.sharding import PartitionSpec as P

norm_eps = 1e-06
MESH = pl.DeviceIdType.MESH
f32 = jnp.float32
bf16 = jnp.bfloat16


def inner_size(dp):
    return max(n for n in range(1, dp + 1) if dp % n == 0 and n * n <= dp)


def kernel(
    dp,
    tensor,
    logit_ref,
    perm_ref,
    clip_hbm,
    proj_hbm,
    cap_hbm,
    clip_grad_ref,
    cap_grad_ref,
    loss_ref,
    clip_v,
    proj_v,
    cap_v,
    part_send,
    part_recv,
    caps,
    vids,
    stats,
    loss_v,
    vid_send,
    vid_recv,
    cap_send,
    cap_recv,
    raw_all,
    load_sem,
    part_ss,
    part_rs,
    caps_ss,
    caps_rs,
    vids_ss,
    vids_rs,
    stats_ss,
    stats_rs,
    vg_ss,
    vg_rs,
    cg_ss,
    cg_rs,
    raw_ss,
    raw_rs,
):
    inner = inner_size(dp)
    na = dp // inner
    nb = inner * tensor
    rows, feats = clip_v.shape
    vrow = rows // tensor
    ccol, width = cap_v.shape
    d = lax.axis_index("dp")
    t = lax.axis_index("tensor")
    a = lax.div(d, inner)
    i = lax.rem(d, inner)
    b = i * tensor + t

    def row_peer(k):
        pb = lax.rem(b + k, nb)
        return pb, (a * inner + lax.div(pb, tensor), lax.rem(pb, tensor))

    def col_peer(k):
        pa = lax.rem(a + k, na)
        return pa, (pa * inner + i, t)

    def tensor_peer(k):
        pt = lax.rem(t + k, tensor)
        return pt, (d, pt)

    def remote(src, dst, ss, rs, device):
        return pltpu.make_async_remote_copy(
            src_ref=src, dst_ref=dst, send_sem=ss, recv_sem=rs, device_id=device, device_id_type=MESH
        )

    load_clip = pltpu.make_async_copy(clip_hbm, clip_v, load_sem.at[0])
    load_proj = pltpu.make_async_copy(proj_hbm, proj_v, load_sem.at[1])
    load_cap = pltpu.make_async_copy(cap_hbm, cap_v, load_sem.at[2])
    load_clip.start()
    load_proj.start()
    load_cap.start()
    barrier = pltpu.get_barrier_semaphore()
    for k in range(1, nb):
        pl.semaphore_signal(barrier, inc=1, device_id=row_peer(k)[1], device_id_type=MESH)
    for k in range(1, na):
        pl.semaphore_signal(barrier, inc=1, device_id=col_peer(k)[1], device_id_type=MESH)

    logit = logit_ref[0]
    sends = []

    load_clip.wait()
    load_proj.wait()
    part_send[...] = jnp.dot(clip_v[...], proj_v[...], preferred_element_type=f32).reshape(tensor, vrow, width)
    pl.semaphore_wait(barrier, nb + na - 2)
    part_copies = []
    for k in range(1, tensor):
        pt, dev = tensor_peer(k)
        c = remote(part_send.at[pt], part_recv.at[k - 1], part_ss.at[k - 1], part_rs.at[k - 1], dev)
        c.start()
        part_copies.append(c)

    load_cap.wait()
    cap_f = cap_v[...].astype(f32)
    cap_inv = lax.rsqrt(jnp.sum(cap_f * cap_f, axis=1, keepdims=True) + norm_eps)
    caps[a] = (cap_f * cap_inv).astype(bf16)
    cap_copies = []
    for k in range(1, na):
        pa, dev = col_peer(k)
        c = remote(caps.at[a], caps.at[a], caps_ss.at[k - 1], caps_rs.at[k - 1], dev)
        c.start()
        cap_copies.append(c)

    raw_proj = part_send[t]
    for k in range(1, tensor):
        part_copies[k - 1].wait_recv()
        raw_proj = raw_proj + part_recv[k - 1]
    vid_inv = lax.rsqrt(jnp.sum(raw_proj * raw_proj, axis=1, keepdims=True) + norm_eps)
    unit_vid = raw_proj * vid_inv
    vids[b] = unit_vid.astype(bf16)
    vid_copies = []
    for k in range(1, nb):
        pb, dev = row_peer(k)
        c = remote(vids.at[b], vids.at[b], vids_ss.at[k - 1], vids_rs.at[k - 1], dev)
        c.start()
        vid_copies.append(c)
    for c in cap_copies:
        c.wait_recv()
    for c in vid_copies:
        c.wait_recv()

    captions = caps[...].reshape(na * ccol, width)
    videos = vids[...].reshape(nb * vrow, width)
    tile_rows = nb * vrow
    scores = logit * lax.dot_general(captions, videos, (((1,), (1,)), ((), ())), preferred_element_type=f32)
    wanted = perm_ref[:, pl.ds(pl.multiple_of(a * tile_rows, tile_rows), tile_rows)]
    index = lax.broadcasted_iota(jnp.int32, (na * ccol, 1), 0)
    column = (index // ccol) * (nb * ccol) + b * ccol + index % ccol
    hit = column == wanted
    top = jnp.max(scores, axis=0, keepdims=True)
    expo = jnp.exp(scores - top)
    total = jnp.sum(expo, axis=0, keepdims=True)
    positive = jnp.sum(jnp.where(hit, scores, 0.0), axis=0, keepdims=True)
    slot = lax.broadcasted_iota(jnp.int32, (8, tile_rows), 0)
    stats[b] = jnp.where(slot == 0, top, jnp.where(slot == 1, total, positive))
    stat_copies = []
    for k in range(1, nb):
        pb, dev = row_peer(k)
        c = remote(stats.at[b], stats.at[b], stats_ss.at[k - 1], stats_rs.at[k - 1], dev)
        c.start()
        stat_copies.append(c)
    for c in stat_copies:
        c.wait_recv()
    every = stats[...]
    row_max = jnp.max(every[:, 0:1, :], axis=0)
    row_sum = jnp.sum(every[:, 1:2, :] * jnp.exp(every[:, 0:1, :] - row_max[None]), axis=0)
    row_pos = jnp.sum(every[:, 2:3, :], axis=0)
    scale = jnp.exp(top - row_max) / row_sum
    weights = (expo * scale - hit.astype(f32)).astype(bf16)

    vid_part = lax.dot_general(weights, captions, (((0,), (0,)), ((), ())), preferred_element_type=f32)
    vid_send[...] = vid_part.astype(bf16).reshape(nb, vrow, width)
    vg_copies = []
    for k in range(1, nb):
        pb, dev = row_peer(k)
        c = remote(vid_send.at[pb], vid_recv.at[k - 1], vg_ss.at[k - 1], vg_rs.at[k - 1], dev)
        c.start()
        vg_copies.append(c)
    cap_part = jnp.dot(weights, videos, preferred_element_type=f32)
    cap_send[...] = cap_part.astype(bf16).reshape(na, ccol, width)
    cg_copies = []
    for k in range(1, na):
        pa, dev = col_peer(k)
        c = remote(cap_send.at[pa], cap_recv.at[k - 1], cg_ss.at[k - 1], cg_rs.at[k - 1], dev)
        c.start()
        cg_copies.append(c)
    loss_v[...] = row_max + jnp.log(row_sum) - row_pos
    loss_ref[...] = loss_v[:, pl.ds(pl.multiple_of(i * rows, rows), rows)]

    vid_grad = vid_send[b].astype(f32)
    for k in range(1, nb):
        vg_copies[k - 1].wait_recv()
        vid_grad = vid_grad + vid_recv[k - 1].astype(f32)
    vid_grad = logit * vid_grad
    vid_dot = jnp.sum(unit_vid * vid_grad, axis=1, keepdims=True)
    raw_all[t] = ((vid_grad - unit_vid * vid_dot) * vid_inv).astype(bf16)
    raw_copies = []
    for k in range(1, tensor):
        pt, dev = tensor_peer(k)
        c = remote(raw_all.at[t], raw_all.at[t], raw_ss.at[k - 1], raw_rs.at[k - 1], dev)
        c.start()
        raw_copies.append(c)

    cap_grad = cap_send[a].astype(f32)
    for k in range(1, na):
        cg_copies[k - 1].wait_recv()
        cap_grad = cap_grad + cap_recv[k - 1].astype(f32)
    cap_grad = logit * cap_grad
    cap_unit = cap_f * cap_inv
    cap_dot = jnp.sum(cap_unit * cap_grad, axis=1, keepdims=True)
    cap_grad_ref[...] = (cap_grad - cap_unit * cap_dot) * cap_inv

    for c in raw_copies:
        c.wait_recv()
    clip_grad_ref[...] = lax.dot_general(
        raw_all[...].reshape(rows, width), proj_v[...], (((1,), (1,)), ((), ())), preferred_element_type=f32
    )
    for group in (part_copies, cap_copies, vid_copies, stat_copies, vg_copies, cg_copies, raw_copies):
        for c in group:
            c.wait_send()


def body(dp, tensor, clip_feats, proj_weight, caption_emb, logit_scale, pair_perm):
    rows, feats = clip_feats.shape
    ccol, width = caption_emb.shape
    inner = inner_size(dp)
    na, nb = dp // inner, inner * tensor
    vrow = rows // tensor
    vmem = pl.BlockSpec(memory_space=pltpu.VMEM)
    anywhere = pl.BlockSpec(memory_space=pl.ANY)
    dma = pltpu.SemaphoreType.DMA
    nr, nc, nt = max(nb - 1, 1), max(na - 1, 1), max(tensor - 1, 1)
    clip_grad, caption_grad, losses = pl.pallas_call(
        functools.partial(kernel, dp, tensor),
        out_shape=(
            jax.ShapeDtypeStruct((rows, feats), f32),
            jax.ShapeDtypeStruct((ccol, width), f32),
            jax.ShapeDtypeStruct((1, rows), f32),
        ),
        in_specs=[pl.BlockSpec(memory_space=pltpu.SMEM), vmem, anywhere, anywhere, anywhere],
        out_specs=(vmem, vmem, vmem),
        scratch_shapes=[
            pltpu.VMEM((rows, feats), bf16),
            pltpu.VMEM(proj_weight.shape, bf16),
            pltpu.VMEM((ccol, width), bf16),
            pltpu.VMEM((tensor, vrow, width), f32),
            pltpu.VMEM((nt, vrow, width), f32),
            pltpu.VMEM((na, ccol, width), bf16),
            pltpu.VMEM((nb, vrow, width), bf16),
            pltpu.VMEM((nb, 8, nb * vrow), f32),
            pltpu.VMEM((1, nb * vrow), f32),
            pltpu.VMEM((nb, vrow, width), bf16),
            pltpu.VMEM((nr, vrow, width), bf16),
            pltpu.VMEM((na, ccol, width), bf16),
            pltpu.VMEM((nc, ccol, width), bf16),
            pltpu.VMEM((tensor, vrow, width), bf16),
            dma((3,)),
            dma((nt,)),
            dma((nt,)),
            dma((nc,)),
            dma((nc,)),
            dma((nr,)),
            dma((nr,)),
            dma((nr,)),
            dma((nr,)),
            dma((nr,)),
            dma((nr,)),
            dma((nc,)),
            dma((nc,)),
            dma((nt,)),
            dma((nt,)),
        ],
        compiler_params=pltpu.CompilerParams(
            collective_id=0, has_side_effects=True, vmem_limit_bytes=48 * 1024 * 1024
        ),
        name="contrastive_step",
    )(logit_scale, pair_perm.reshape(1, -1), clip_feats, proj_weight, caption_emb)
    return clip_grad, caption_grad, losses.reshape(rows)


def solution(mesh):
    return jax.shard_map(
        functools.partial(body, mesh.shape["dp"], mesh.shape["tensor"]),
        mesh=mesh,
        in_specs=(P("dp", "tensor"), P("tensor", None), P(("dp", "tensor"), None), P(), P()),
        out_specs=(P("dp", "tensor"), P(("dp", "tensor"), None), P("dp")),
        check_vma=False,
    )
```

time: 144 us -> 41 us (0.28)
  waiting for transfers between devices: 98 us -> 0 us
  Pallas kernels: 0 us -> 34 us
  between operations: 16.2 us -> 1.3 us
  blocking collectives: 10 us -> 0 us
  other arithmetic: 9.03 us -> 0 us
  matrix products: 8.93 us -> 0 us
  local copies, waits for them, and re-layouts: 1.05 us -> 5.42 us
    psum x2 -> x0, waiting for transfers between devices: 42.6 us -> none  [the longest x1 22.6 us: body(): raw_proj = lax.psum(partial_value, 'tensor')]
    reduce_scatter x1 -> x0, waiting for transfers between devices: 39.4 us -> none  [body(): cap_grad = lax.psum_scatter(cap_part, 'dp', scatter_dimension=0, tiled=True)]
    pallas_call x0 -> x1, Pallas kernels: none -> 34 us  [body(): pl.pallas_call(functools.partial(kernel, dp, tensor), out_shape=(jax.Shap...]
    all_gather x1 -> x0, waiting for transfers between devices: 16 us -> none  [body(): gathered = lax.all_gather(captions, 'dp', axis=0, tiled=True)]
    dot_general x5 -> x0, matrix products: 8.93 us -> none  [the longest x1 2.05 us: body(): lax.dot_general(raw_grad, proj_weight, (((1,), (1,)), ((), ())), preferre...]
    pmax x1 -> x0, blocking collectives: 5.07 us -> none  [body(): row_max = lax.pmax(stats[0], 'tensor')]
    psum x1 -> x0, blocking collectives: 4.93 us -> none  [body(): lax.psum((stats[1] * jnp.exp(stats[0] - row_max), stats[2]), 'tensor')]
    reduce_sum x5 -> x0, other arithmetic: 4.48 us -> none  [the longest x2 2.01 us: unit_rows(): squares = jnp.sum(values * values, axis=1, keepdims=True)]
  transfers between devices with their start and end apart: 4 -> 0, of which waited for: 4 -> 0; matrix products, arithmetic and copies ran while one was open for 7% -> 0% of each run, Pallas kernels for 0% -> 0%
where the time goes in v1:
time: 41 us; the launch traced here: 40.7 us
  Pallas kernels  34 us (83%)
  local copies, waits for them, and re-layouts  5.42 us (13%)
  between operations  1.3 us (3%)
    pallas_call x1, Pallas kernels, body(): pl.pallas_call(functools.partial(kernel, dp, tensor), out_shape=(jax.Shap...  34 us
    unnamed x11, local copies, waits for them, and re-layouts  5.42 us

profile of v1, /device:TPU:0, one launch (start us, length us, event | category | flops | bytes accessed | tf_op | source)
XLA Modules:
  0.0 40.7 jit_solution(2492694430813779990)
XLA Ops:
  1.3 0.0 copy-start
  1.3 1.1 %copy-done = bf16[640,512]{1,0:T(8,128)(2,1)S(1)} copy-done((bf16[640,512]{1,0:T(8,128)(2,1)S(1)}, bf16[640,512]{1,0:T(8,128)(2,1)}, u32[]{:S(2)}) %copy-start) | copy-done | bytes 655384
  2.4 0.0 copy-start.1
  2.4 0.9 %copy-done.1 = bf16[128,640]{1,0:T(8,128)(2,1)S(1)} copy-done((bf16[128,640]{1,0:T(8,128)(2,1)S(1)}, bf16[128,640]{1,0:T(8,128)(2,1)}, u32[]{:S(2)}) %copy-start.1) | copy-done | bytes 163864
  3.3 0.0 copy-start.2
  3.3 0.8 %copy-done.2 = bf16[64,512]{1,0:T(8,128)(2,1)S(1)} copy-done((bf16[64,512]{1,0:T(8,128)(2,1)S(1)}, bf16[64,512]{1,0:T(8,128)(2,1)}, u32[]{:S(2)}) %copy-start.2) | copy-done | bytes 65560
  4.1 0.0 copy-start.3
  4.1 0.7 %copy-done.3 = s32[2048]{0:T(1024)S(1)} copy-done((s32[2048]{0:T(1024)S(1)}, s32[2048]{0:T(1024)}, u32[]{:S(2)}) %copy-start.3) | copy-done | bytes 8216
  4.8 34.0 %contrastive_step.1 = (f32[128,640]{1,0:T(8,128)S(1)}, f32[64,512]{1,0:T(8,128)S(1)}, f32[1,128]{1,0:T(1,128)S(1)}) custom-call(f32[1]{0:T(128)S(6)} %copy.11.logit_ref, s32[1,2048]{1,0:T(1,128)S(1)} %bitcast.2, bf16[128,640]{1,0:T(8,128)(2,1)S(1)} %copy-done.1, bf16[640,512]{1,0:T(8,128)(2,1)S(1)} %copy-done, bf16[64,512]{1,0:T(8,128)(2,1)S(1)} %copy-done.2), custom_call_target="tpu_custom_call" | custom-call | tf_op jit(solution)/shard_map/contrastive_step/pallas_call | solution.py:236
  38.8 0.7 %copy.12 = f32[128,640]{1,0:T(8,128)} copy(f32[128,640]{1,0:T(8,128)S(1)} %get-tuple-element.12) | data formatting | bytes 655360
  39.5 0.7 %copy.13 = f32[64,512]{1,0:T(8,128)} copy(f32[64,512]{1,0:T(8,128)S(1)} %get-tuple-element.13) | data formatting | bytes 262144
  40.2 0.5 %copy.14 = f32[128]{0:T(128)} copy(f32[128]{0:T(128)S(1)} %bitcast.3) | data formatting | bytes 1024
Async XLA Ops:
  1.3 1.1 %copy-start = (bf16[640,512]{1,0:T(8,128)(2,1)S(1)}, bf16[640,512]{1,0:T(8,128)(2,1)}, u32[]{:S(2)}) copy-start(bf16[640,512]{1,0:T(8,128)(2,1)} %proj_hbm.1) | copy-start | bytes 1966084
  2.4 0.9 %copy-start.1 = (bf16[128,640]{1,0:T(8,128)(2,1)S(1)}, bf16[128,640]{1,0:T(8,128)(2,1)}, u32[]{:S(2)}) copy-start(bf16[128,640]{1,0:T(8,128)(2,1)} %clip_hbm.1) | copy-start | bytes 491524
  3.3 0.8 %copy-start.2 = (bf16[64,512]{1,0:T(8,128)(2,1)S(1)}, bf16[64,512]{1,0:T(8,128)(2,1)}, u32[]{:S(2)}) copy-start(bf16[64,512]{1,0:T(8,128)(2,1)} %cap_hbm.1) | copy-start | bytes 196612
  4.1 0.7 %copy-start.3 = (s32[2048]{0:T(1024)S(1)}, s32[2048]{0:T(1024)}, u32[]{:S(2)}) copy-start(s32[2048]{0:T(1024)} %param.9) | copy-start | bytes 24580

commit v2 on v1

v2 whole, which is shorter than its diff:
```python
import functools

import jax
import jax.numpy as jnp
from jax import lax
from jax.experimental import pallas as pl
from jax.experimental.pallas import tpu as pltpu
from jax.sharding import PartitionSpec as P

norm_eps = 1e-06
MESH = pl.DeviceIdType.MESH
f32 = jnp.float32
bf16 = jnp.bfloat16


def split(dp):
    pair = 2 if dp % 2 == 0 else 1
    rest = dp // pair
    inner = max(n for n in range(1, rest + 1) if rest % n == 0 and n * n <= rest)
    return rest // inner, inner, pair


def kernel(
    dp,
    tensor,
    logit_ref,
    perm_hbm,
    clip_hbm,
    proj_hbm,
    cap_hbm,
    clip_grad_ref,
    cap_grad_ref,
    loss_ref,
    perm_v,
    clip_v,
    proj_v,
    cap_v,
    part_send,
    part_recv,
    caps,
    vids,
    stats,
    loss_v,
    weights_v,
    cap_acc,
    vid_send,
    vid_recv,
    pre_send,
    pre_recv,
    cap_send,
    cap_recv,
    raw_all,
    load_sem,
    part_ss,
    part_rs,
    caps_ss,
    caps_rs,
    fwd_ss,
    fwd_rs,
    vids_ss,
    vids_rs,
    stats_ss,
    stats_rs,
    vg_ss,
    vg_rs,
    pre_ss,
    pre_rs,
    cg_ss,
    cg_rs,
    raw_ss,
    raw_rs,
):
    outer, inner, pair = split(dp)
    nb = inner * tensor
    rows, feats = clip_v.shape
    vrow = rows // tensor
    ccol, width = cap_v.shape
    tile_cols = outer * pair * ccol
    tile_rows = nb * vrow
    d = lax.axis_index("dp")
    t = lax.axis_index("tensor")
    c = lax.rem(d, pair)
    i = lax.rem(lax.div(d, pair), inner)
    z = lax.div(d, pair * inner)
    b = i * tensor + t

    def dp_index(zz, ii, cc):
        return (zz * inner + ii) * pair + cc

    def row_peer(k):
        pb = lax.rem(b + k, nb)
        return pb, (dp_index(z, lax.div(pb, tensor), c), lax.rem(pb, tensor))

    def col_peer(k):
        pz = lax.rem(z + k, outer)
        return pz, (dp_index(pz, i, c), t)

    def core_peer():
        return (dp_index(z, i, pair - 1 - c), t)

    def tensor_peer(k):
        pt = lax.rem(t + k, tensor)
        return pt, (d, pt)

    started = []

    def send(src, dst, ss, rs, device):
        copy = pltpu.make_async_remote_copy(
            src_ref=src, dst_ref=dst, send_sem=ss, recv_sem=rs, device_id=device, device_id_type=MESH
        )
        copy.start()
        started.append(copy)
        return copy

    loads = [
        pltpu.make_async_copy(src, dst, load_sem.at[n])
        for n, (src, dst) in enumerate(((proj_hbm, proj_v), (clip_hbm, clip_v), (cap_hbm, cap_v), (perm_hbm, perm_v)))
    ]
    for load in loads:
        load.start()
    barrier = pltpu.get_barrier_semaphore()
    peers = [row_peer(k)[1] for k in range(1, nb)] + [col_peer(k)[1] for k in range(1, outer)]
    if pair > 1:
        peers.append(core_peer())
    for device in peers:
        pl.semaphore_signal(barrier, inc=1, device_id=device, device_id_type=MESH)
    logit = logit_ref[0]

    loads[0].wait()
    loads[1].wait()
    part_send[...] = jnp.dot(clip_v[...], proj_v[...], preferred_element_type=f32).reshape(tensor, vrow, width)
    loads[2].wait()
    loads[3].wait()
    cap_f = cap_v[...].astype(f32)
    cap_inv = lax.rsqrt(jnp.sum(cap_f * cap_f, axis=1, keepdims=True) + norm_eps)
    caps[c, z] = (cap_f * cap_inv).astype(bf16)
    pl.semaphore_wait(barrier, len(peers))
    part_copies = []
    for k in range(1, tensor):
        pt, dev = tensor_peer(k)
        part_copies.append(send(part_send.at[pt], part_recv.at[k - 1], part_ss.at[k - 1], part_rs.at[k - 1], dev))
    cap_copies = []
    for k in range(1, outer):
        pz, dev = col_peer(k)
        cap_copies.append(send(caps.at[c, z], caps.at[c, z], caps_ss.at[k - 1], caps_rs.at[k - 1], dev))
    fwd_copies = []
    if pair > 1:
        fwd_copies.append(send(caps.at[c, z], caps.at[c, z], fwd_ss.at[0], fwd_rs.at[0], core_peer()))

    raw_proj = part_send[t]
    for k in range(1, tensor):
        part_copies[k - 1].wait_recv()
        raw_proj = raw_proj + part_recv[k - 1]
    vid_inv = lax.rsqrt(jnp.sum(raw_proj * raw_proj, axis=1, keepdims=True) + norm_eps)
    unit_vid = raw_proj * vid_inv
    vids[b] = unit_vid.astype(bf16)
    vid_copies = []
    for k in range(1, nb):
        pb, dev = row_peer(k)
        vid_copies.append(send(vids.at[b], vids.at[b], vids_ss.at[k - 1], vids_rs.at[k - 1], dev))
    for k in range(1, outer):
        cap_copies[k - 1].wait_recv()
        if pair > 1:
            pz = lax.rem(z + (outer - k), outer)
            fwd_copies.append(send(caps.at[c, pz], caps.at[c, pz], fwd_ss.at[k], fwd_rs.at[k], core_peer()))
    for copy in fwd_copies:
        copy.wait_recv()
    for copy in vid_copies:
        copy.wait_recv()

    captions = caps[...].reshape(tile_cols, width)
    videos = vids[...].reshape(tile_rows, width)
    scores = logit * lax.dot_general(captions, videos, (((1,), (1,)), ((), ())), preferred_element_type=f32)
    wanted = jnp.concatenate(
        [perm_v[:, pl.ds(pl.multiple_of(dp_index(z, n, c) * rows, rows), rows)] for n in range(inner)], axis=1
    )
    index = lax.broadcasted_iota(jnp.int32, (tile_cols, 1), 0)
    block = index // ccol
    column = (dp_index(block % outer, i, block // outer) * tensor + t) * ccol + index % ccol
    hit = column == wanted
    top = jnp.max(scores, axis=0, keepdims=True)
    expo = jnp.exp(scores - top)
    total = jnp.sum(expo, axis=0, keepdims=True)
    positive = jnp.sum(jnp.where(hit, scores, 0.0), axis=0, keepdims=True)
    stats[b] = jnp.concatenate([top, total, positive], axis=1)
    stat_copies = []
    for k in range(1, nb):
        pb, dev = row_peer(k)
        stat_copies.append(send(stats.at[b], stats.at[b], stats_ss.at[k - 1], stats_rs.at[k - 1], dev))
    for copy in stat_copies:
        copy.wait_recv()
    every = [stats[n] for n in range(nb)]
    tops = [v[:, :tile_rows] for v in every]
    row_max = functools.reduce(jnp.maximum, tops)
    row_sum = functools.reduce(
        jnp.add, [v[:, tile_rows : 2 * tile_rows] * jnp.exp(m - row_max) for v, m in zip(every, tops)]
    )
    row_pos = functools.reduce(jnp.add, [v[:, 2 * tile_rows :] for v in every])
    scale = jnp.exp(top - row_max) / row_sum
    weights = (expo * scale - hit.astype(f32)).astype(bf16)
    weights_v[...] = weights.reshape(pair, outer * ccol, tile_rows)

    pre_copies = []
    if pair > 1:
        part = jnp.dot(weights_v[pair - 1 - c], videos, preferred_element_type=f32)
        pre_send[...] = part.astype(bf16).reshape(outer, ccol, width)
        for k in range(outer):
            pz = lax.rem(z + k + 1, outer)
            pre_copies.append(send(pre_send.at[pz], pre_recv.at[k], pre_ss.at[k], pre_rs.at[k], core_peer()))
    vid_part = lax.dot_general(weights, captions, (((0,), (0,)), ((), ())), preferred_element_type=f32)
    vid_send[...] = vid_part.astype(bf16).reshape(nb, vrow, width)
    vg_copies = []
    for k in range(1, nb):
        pb, dev = row_peer(k)
        vg_copies.append(send(vid_send.at[pb], vid_recv.at[k - 1], vg_ss.at[k - 1], vg_rs.at[k - 1], dev))
    own = jnp.dot(weights_v[c], videos, preferred_element_type=f32)
    cap_acc[...] = own.reshape(outer, ccol, width)
    cg_copies = []
    for k in range(outer):
        pz = lax.rem(z + k + 1, outer)
        block_sum = cap_acc[pz]
        if pair > 1:
            pre_copies[k].wait_recv()
            block_sum = block_sum + pre_recv[k].astype(f32)
        if k < outer - 1:
            cap_send[k] = block_sum.astype(bf16)
            cg_copies.append(send(cap_send.at[k], cap_recv.at[k], cg_ss.at[k], cg_rs.at[k], col_peer(k + 1)[1]))
    cap_grad = block_sum
    loss_v[...] = row_max + jnp.log(row_sum) - row_pos
    loss_ref[...] = loss_v[:, pl.ds(pl.multiple_of(i * rows, rows), rows)]

    vid_grad = vid_send[b].astype(f32)
    for k in range(1, nb):
        vg_copies[k - 1].wait_recv()
        vid_grad = vid_grad + vid_recv[k - 1].astype(f32)
    vid_grad = logit * vid_grad
    vid_dot = jnp.sum(unit_vid * vid_grad, axis=1, keepdims=True)
    raw_all[t] = ((vid_grad - unit_vid * vid_dot) * vid_inv).astype(bf16)
    raw_copies = []
    for k in range(1, tensor):
        pt, dev = tensor_peer(k)
        raw_copies.append(send(raw_all.at[t], raw_all.at[t], raw_ss.at[k - 1], raw_rs.at[k - 1], dev))

    for k in range(outer - 1):
        cg_copies[k].wait_recv()
        cap_grad = cap_grad + cap_recv[k].astype(f32)
    cap_grad = logit * cap_grad
    cap_unit = cap_f * cap_inv
    cap_dot = jnp.sum(cap_unit * cap_grad, axis=1, keepdims=True)
    cap_grad_ref[...] = (cap_grad - cap_unit * cap_dot) * cap_inv

    for copy in raw_copies:
        copy.wait_recv()
    clip_grad_ref[...] = lax.dot_general(
        raw_all[...].reshape(rows, width), proj_v[...], (((1,), (1,)), ((), ())), preferred_element_type=f32
    )
    for copy in started:
        copy.wait_send()


def body(dp, tensor, clip_feats, proj_weight, caption_emb, logit_scale, pair_perm):
    rows, feats = clip_feats.shape
    ccol, width = caption_emb.shape
    outer, inner, pair = split(dp)
    nb = inner * tensor
    vrow = rows // tensor
    tile_rows = nb * vrow
    vmem = pl.BlockSpec(memory_space=pltpu.VMEM)
    hbm = pl.BlockSpec(memory_space=pltpu.HBM)
    dma = pltpu.SemaphoreType.DMA
    nr, no, nt = max(nb - 1, 1), max(outer - 1, 1), max(tensor - 1, 1)
    clip_grad, caption_grad, losses = pl.pallas_call(
        functools.partial(kernel, dp, tensor),
        out_shape=(
            jax.ShapeDtypeStruct((rows, feats), f32),
            jax.ShapeDtypeStruct((ccol, width), f32),
            jax.ShapeDtypeStruct((1, rows), f32),
        ),
        in_specs=[pl.BlockSpec(memory_space=pltpu.SMEM), hbm, hbm, hbm, hbm],
        out_specs=(vmem, vmem, vmem),
        scratch_shapes=[
            pltpu.VMEM((1, pair_perm.shape[0]), jnp.int32),
            pltpu.VMEM((rows, feats), bf16),
            pltpu.VMEM(proj_weight.shape, bf16),
            pltpu.VMEM((ccol, width), bf16),
            pltpu.VMEM((tensor, vrow, width), f32),
            pltpu.VMEM((nt, vrow, width), f32),
            pltpu.VMEM((pair, outer, ccol, width), bf16),
            pltpu.VMEM((nb, vrow, width), bf16),
            pltpu.VMEM((nb, 1, 3 * tile_rows), f32),
            pltpu.VMEM((1, tile_rows), f32),
            pltpu.VMEM((pair, outer * ccol, tile_rows), bf16),
            pltpu.VMEM((outer, ccol, width), f32),
            pltpu.VMEM((nb, vrow, width), bf16),
            pltpu.VMEM((nr, vrow, width), bf16),
            pltpu.VMEM((outer, ccol, width), bf16),
            pltpu.VMEM((outer, ccol, width), bf16),
            pltpu.VMEM((no, ccol, width), bf16),
            pltpu.VMEM((no, ccol, width), bf16),
            pltpu.VMEM((tensor, vrow, width), bf16),
            dma((4,)),
            *[dma((nt,))] * 2,
            *[dma((no,))] * 2,
            *[dma((outer,))] * 2,
            *[dma((nr,))] * 2,
            *[dma((nr,))] * 2,
            *[dma((nr,))] * 2,
            *[dma((outer,))] * 2,
            *[dma((no,))] * 2,
            *[dma((nt,))] * 2,
        ],
        compiler_params=pltpu.CompilerParams(collective_id=0, has_side_effects=True, vmem_limit_bytes=67043328),
        name="contrastive_step",
    )(logit_scale, pair_perm.reshape(1, -1), clip_feats, proj_weight, caption_emb)
    return clip_grad, caption_grad, losses.reshape(rows)


def solution(mesh):
    return jax.shard_map(
        functools.partial(body, mesh.shape["dp"], mesh.shape["tensor"]),
        mesh=mesh,
        in_specs=(P("dp", "tensor"), P("tensor", None), P(("dp", "tensor"), None), P(), P()),
        out_specs=(P("dp", "tensor"), P(("dp", "tensor"), None), P("dp")),
        check_vma=False,
    )
```

time: 41 us -> 33.6 us (0.82)
  Pallas kernels: 34 us -> 29.2 us
  local copies, waits for them, and re-layouts: 5.42 us -> 2.93 us
    pallas_call x1, Pallas kernels: 34 us -> 29.2 us  [body(): pl.pallas_call(functools.partial(kernel, dp, tensor), out_shape=(jax.Shap...]
    unnamed x11 -> x7, local copies, waits for them, and re-layouts: 5.42 us -> 2.93 us
where the time goes in v2:
time: 33.6 us; the launch traced here: 33.4 us
  Pallas kernels  29.2 us (87%)
  local copies, waits for them, and re-layouts  2.93 us (9%)
  between operations  1.3 us (4%)
    pallas_call x1, Pallas kernels, body(): pl.pallas_call(functools.partial(kernel, dp, tensor), out_shape=(jax.Shap...  29.2 us
    unnamed x7, local copies, waits for them, and re-layouts  2.93 us

profile of v2, /device:TPU:0, one launch (start us, length us, event | category | flops | bytes accessed | tf_op | source)
XLA Modules:
  0.0 33.4 jit_solution(2559103338999094129)
XLA Ops:
  1.3 29.2 %contrastive_step.1 = (f32[128,640]{1,0:T(8,128)}, f32[64,512]{1,0:T(8,128)}, f32[1,128]{1,0:T(1,128)}) custom-call(f32[1]{0:T(128)S(6)} %copy.11.logit_ref, s32[1,2048]{1,0:T(1,128)} %bitcast.2, bf16[128,640]{1,0:T(8,128)(2,1)} %clip_hbm.1, bf16[640,512]{1,0:T(8,128)(2,1)} %proj_hbm.1, bf16[64,512]{1,0:T(8,128)(2,1)} %cap_hbm.1), custom_call_target="tpu_custom_call" | custom-call | tf_op jit(solution)/shard_map/contrastive_step/pallas_call | solution.py:272
  30.5 0.0 copy-start
  30.5 1.8 %copy.12 = f32[128,640]{1,0:T(8,128)} copy(f32[128,640]{1,0:T(8,128)} %get-tuple-element.12) | data formatting | bytes 655360
  32.3 0.0 copy-done
  32.3 0.0 copy-start.1
  32.3 0.7 %copy.13 = f32[64,512]{1,0:T(8,128)} copy(f32[64,512]{1,0:T(8,128)S(1)} %copy-done) | data formatting | bytes 262144
  32.9 0.0 copy-done.1
  32.9 0.5 %copy.14 = f32[128]{0:T(128)} copy(f32[128]{0:T(128)S(1)} %bitcast.3) | data formatting | bytes 1024
Async XLA Ops:
  30.5 1.8 %copy-start = (f32[64,512]{1,0:T(8,128)S(1)}, f32[64,512]{1,0:T(8,128)}, u32[]{:S(2)}) copy-start(f32[64,512]{1,0:T(8,128)} %get-tuple-element.13) | copy-start | bytes 393220
  32.3 0.7 %copy-start.1 = (f32[1,128]{1,0:T(1,128)S(1)}, f32[1,128]{1,0:T(1,128)}, u32[]{:S(2)}) copy-start(f32[1,128]{1,0:T(1,128)} %get-tuple-element.8) | copy-start | bytes 1540

commit v3 on v2

--- a/solution.py
+++ b/solution.py
@@ -258,6 +258,28 @@
         copy.wait_send()
 
 
+def store_kernel(*refs):
+    count = len(refs) // 2
+    sems = refs[-1]
+    copies = [pltpu.make_async_copy(refs[n], refs[count + n], sems.at[n]) for n in range(count)]
+    for copy in copies:
+        copy.start()
+    for copy in copies:
+        copy.wait()
+
+
+def store_results(*values):
+    return pl.pallas_call(
+        store_kernel,
+        out_shape=tuple(jax.ShapeDtypeStruct(v.shape, v.dtype) for v in values),
+        in_specs=[pl.BlockSpec(memory_space=pltpu.VMEM)] * len(values),
+        out_specs=tuple(pl.BlockSpec(memory_space=pltpu.HBM) for v in values),
+        scratch_shapes=[pltpu.SemaphoreType.DMA((len(values),))],
+        compiler_params=pltpu.CompilerParams(vmem_limit_bytes=4 * 1024 * 1024),
+        name="store_results",
+    )(*values)
+
+
 def body(dp, tensor, clip_feats, proj_weight, caption_emb, logit_scale, pair_perm):
     rows, feats = clip_feats.shape
     ccol, width = caption_emb.shape
@@ -309,9 +331,10 @@
             *[dma((no,))] * 2,
             *[dma((nt,))] * 2,
         ],
-        compiler_params=pltpu.CompilerParams(collective_id=0, has_side_effects=True, vmem_limit_bytes=67043328),
+        compiler_params=pltpu.CompilerParams(collective_id=0, has_side_effects=True, vmem_limit_bytes=48 * 1024 * 1024),
         name="contrastive_step",
-    )(logit_scale, pair_perm.reshape(1, -1), clip_feats, proj_weight, caption_emb)
+    )(logit_scale, *[pltpu.with_memory_space_constraint(x, pltpu.HBM) for x in (pair_perm.reshape(1, -1), clip_feats, proj_weight, caption_emb)])
+    clip_grad, caption_grad, losses = store_results(clip_grad, caption_grad, losses)
     return clip_grad, caption_grad, losses.reshape(rows)
 
 

time: 33.6 us -> 30.7 us (0.914)
  local copies, waits for them, and re-layouts: 2.93 us -> 0 us
    unnamed x7 -> x0, local copies, waits for them, and re-layouts: 2.93 us -> none
    pallas_call x0 -> x1, Pallas kernels: none -> 0.79 us  [store_results(): pl.pallas_call(store_kernel, out_shape=tuple((jax.ShapeDtypeStruct(v.shap...]
    pallas_call x1, Pallas kernels: 29.2 us -> 28.4 us  [body(): pl.pallas_call(functools.partial(kernel, dp, tensor), out_shape=(jax.Shap...]
where the time goes in v3:
time: 30.7 us; the launch traced here: 30.5 us
  Pallas kernels  29.2 us (95%)
  between operations  1.29 us (4%)
    pallas_call x1, Pallas kernels, body(): pl.pallas_call(functools.partial(kernel, dp, tensor), out_shape=(jax.Shap...  28.4 us
    pallas_call x1, Pallas kernels, store_results(): pl.pallas_call(store_kernel, out_shape=tuple((jax.ShapeDtypeStruct(v.shap...  0.79 us

profile of v3, /device:TPU:0, one launch (start us, length us, event | category | flops | bytes accessed | tf_op | source)
XLA Modules:
  0.0 30.5 jit_solution(3487628644257601723)
XLA Ops:
  1.3 28.4 %contrastive_step.1 = (f32[128,640]{1,0:T(8,128)S(1)}, f32[64,512]{1,0:T(8,128)S(1)}, f32[1,128]{1,0:T(1,128)S(1)}) custom-call(f32[1]{0:T(128)S(6)} %copy.8.logit_ref, s32[1,2048]{1,0:T(1,128)} %bitcast.2, bf16[128,640]{1,0:T(8,128)(2,1)} %clip_hbm.1, bf16[640,512]{1,0:T(8,128)(2,1)} %proj_hbm.1, bf16[64,512]{1,0:T(8,128)(2,1)} %cap_hbm.1), custom_call_target="tpu_custom_call" | custom-call | tf_op jit(solution)/shard_map/contrastive_step/pallas_call | solution.py:294
  29.7 0.8 %store_results.1 = (f32[128,640]{1,0:T(8,128)}, f32[64,512]{1,0:T(8,128)}, f32[1,128]{1,0:T(1,128)}) custom-call(f32[128,640]{1,0:T(8,128)S(1)} %get-tuple-element.9.refs_0_, f32[64,512]{1,0:T(8,128)S(1)} %get-tuple-element.10.refs_1_, f32[1,128]{1,0:T(1,128)S(1)} %get-tuple-element.11.refs_2_), custom_call_target="tpu_custom_call" | custom-call | tf_op jit(solution)/shard_map/store_results/pallas_call | solution.py:272

commit v4 on v3

--- a/solution.py
+++ b/solution.py
@@ -18,6 +18,10 @@
     rest = dp // pair
     inner = max(n for n in range(1, rest + 1) if rest % n == 0 and n * n <= rest)
     return rest // inner, inner, pair
+
+
+def chunks(vrow):
+    return max(n for n in (1, 2, 2) if vrow % (16 * n) == 0 or n == 1)
 
 
 def kernel(
@@ -76,6 +80,8 @@
     vrow = rows // tensor
     ccol, width = cap_v.shape
     tile_cols = outer * pair * ccol
+    nq = chunks(vrow)
+    pieces = [pl.ds(q * (vrow // nq), vrow // nq) for q in range(nq)]
     tile_rows = nb * vrow
     d = lax.axis_index("dp")
     t = lax.axis_index("tensor")
@@ -124,21 +130,23 @@
         peers.append(core_peer())
     for device in peers:
         pl.semaphore_signal(barrier, inc=1, device_id=device, device_id_type=MESH)
-    logit = logit_ref[0]
 
     loads[0].wait()
     loads[1].wait()
     part_send[...] = jnp.dot(clip_v[...], proj_v[...], preferred_element_type=f32).reshape(tensor, vrow, width)
     loads[2].wait()
     loads[3].wait()
+    logit = logit_ref[0]
     cap_f = cap_v[...].astype(f32)
     cap_inv = lax.rsqrt(jnp.sum(cap_f * cap_f, axis=1, keepdims=True) + norm_eps)
     caps[c, z] = (cap_f * cap_inv).astype(bf16)
     pl.semaphore_wait(barrier, len(peers))
     part_copies = []
-    for k in range(1, tensor):
-        pt, dev = tensor_peer(k)
-        part_copies.append(send(part_send.at[pt], part_recv.at[k - 1], part_ss.at[k - 1], part_rs.at[k - 1], dev))
+    for q, piece in enumerate(pieces):
+        for k in range(1, tensor):
+            pt, dev = tensor_peer(k)
+            src, dst = part_send.at[pt, piece], part_recv.at[k - 1, piece]
+            part_copies.append(send(src, dst, part_ss.at[k - 1, q], part_rs.at[k - 1, q], dev))
     cap_copies = []
     for k in range(1, outer):
         pz, dev = col_peer(k)
@@ -147,18 +155,21 @@
     if pair > 1:
         fwd_copies.append(send(caps.at[c, z], caps.at[c, z], fwd_ss.at[0], fwd_rs.at[0], core_peer()))
 
-    raw_proj = part_send[t]
-    for k in range(1, tensor):
-        part_copies[k - 1].wait_recv()
-        raw_proj = raw_proj + part_recv[k - 1]
-    vid_inv = lax.rsqrt(jnp.sum(raw_proj * raw_proj, axis=1, keepdims=True) + norm_eps)
-    unit_vid = raw_proj * vid_inv
-    vids[b] = unit_vid.astype(bf16)
-    vid_copies = []
-    for k in range(1, nb):
-        pb, dev = row_peer(k)
-        vid_copies.append(send(vids.at[b], vids.at[b], vids_ss.at[k - 1], vids_rs.at[k - 1], dev))
-    for k in range(1, outer):
+    unit_vid, vid_inv, vid_copies = [], [], []
+    for q, piece in enumerate(pieces):
+        raw_proj = part_send[t, piece]
+        for k in range(1, tensor):
+            part_copies[q * (tensor - 1) + k - 1].wait_recv()
+            raw_proj = raw_proj + part_recv[k - 1, piece]
+        inverse = lax.rsqrt(jnp.sum(raw_proj * raw_proj, axis=1, keepdims=True) + norm_eps)
+        vid_inv.append(inverse)
+        unit_vid.append(raw_proj * inverse)
+        vids[b, piece] = unit_vid[q].astype(bf16)
+        for k in range(1, nb):
+            pb, dev = row_peer(k)
+            here = vids.at[b, piece]
+            vid_copies.append(send(here, here, vids_ss.at[k - 1, q], vids_rs.at[k - 1, q], dev))
+    for k in range(outer - 1, 0, -1):
         cap_copies[k - 1].wait_recv()
         if pair > 1:
             pz = lax.rem(z + (outer - k), outer)
@@ -200,6 +211,14 @@
     weights = (expo * scale - hit.astype(f32)).astype(bf16)
     weights_v[...] = weights.reshape(pair, outer * ccol, tile_rows)
 
+    vid_part = lax.dot_general(weights, captions, (((0,), (0,)), ((), ())), preferred_element_type=f32)
+    vid_send[...] = vid_part.astype(bf16).reshape(nb, vrow, width)
+    vg_copies = []
+    for q, piece in enumerate(pieces):
+        for k in range(1, nb):
+            pb, dev = row_peer(k)
+            src, dst = vid_send.at[pb, piece], vid_recv.at[k - 1, piece]
+            vg_copies.append(send(src, dst, vg_ss.at[k - 1, q], vg_rs.at[k - 1, q], dev))
     pre_copies = []
     if pair > 1:
         part = jnp.dot(weights_v[pair - 1 - c], videos, preferred_element_type=f32)
@@ -207,12 +226,6 @@
         for k in range(outer):
             pz = lax.rem(z + k + 1, outer)
             pre_copies.append(send(pre_send.at[pz], pre_recv.at[k], pre_ss.at[k], pre_rs.at[k], core_peer()))
-    vid_part = lax.dot_general(weights, captions, (((0,), (0,)), ((), ())), preferred_element_type=f32)
-    vid_send[...] = vid_part.astype(bf16).reshape(nb, vrow, width)
-    vg_copies = []
-    for k in range(1, nb):
-        pb, dev = row_peer(k)
-        vg_copies.append(send(vid_send.at[pb], vid_recv.at[k - 1], vg_ss.at[k - 1], vg_rs.at[k - 1], dev))
     own = jnp.dot(weights_v[c], videos, preferred_element_type=f32)
     cap_acc[...] = own.reshape(outer, ccol, width)
     cg_copies = []
@@ -226,21 +239,28 @@
             cap_send[k] = block_sum.astype(bf16)
             cg_copies.append(send(cap_send.at[k], cap_recv.at[k], cg_ss.at[k], cg_rs.at[k], col_peer(k + 1)[1]))
     cap_grad = block_sum
+    raw_copies = []
+    for q, piece in enumerate(pieces):
+        vid_grad = vid_send[b, piece].astype(f32)
+        for k in range(1, nb):
+            vg_copies[q * (nb - 1) + k - 1].wait_recv()
+            vid_grad = vid_grad + vid_recv[k - 1, piece].astype(f32)
+        vid_grad = logit * vid_grad
+        vid_dot = jnp.sum(unit_vid[q] * vid_grad, axis=1, keepdims=True)
+        raw_all[t, piece] = ((vid_grad - unit_vid[q] * vid_dot) * vid_inv[q]).astype(bf16)
+        for k in range(1, tensor):
+            pt, dev = tensor_peer(k)
+            here = raw_all.at[t, piece]
+            raw_copies.append(send(here, here, raw_ss.at[k - 1, q], raw_rs.at[k - 1, q], dev))
+
+    def clip_rows(owner):
+        clip_grad_ref[pl.ds(pl.multiple_of(owner * vrow, vrow), vrow), :] = lax.dot_general(
+            raw_all[owner], proj_v[...], (((1,), (1,)), ((), ())), preferred_element_type=f32
+        )
+
+    clip_rows(t)
     loss_v[...] = row_max + jnp.log(row_sum) - row_pos
     loss_ref[...] = loss_v[:, pl.ds(pl.multiple_of(i * rows, rows), rows)]
-
-    vid_grad = vid_send[b].astype(f32)
-    for k in range(1, nb):
-        vg_copies[k - 1].wait_recv()
-        vid_grad = vid_grad + vid_recv[k - 1].astype(f32)
-    vid_grad = logit * vid_grad
-    vid_dot = jnp.sum(unit_vid * vid_grad, axis=1, keepdims=True)
-    raw_all[t] = ((vid_grad - unit_vid * vid_dot) * vid_inv).astype(bf16)
-    raw_copies = []
-    for k in range(1, tensor):
-        pt, dev = tensor_peer(k)
-        raw_copies.append(send(raw_all.at[t], raw_all.at[t], raw_ss.at[k - 1], raw_rs.at[k - 1], dev))
-
     for k in range(outer - 1):
         cg_copies[k].wait_recv()
         cap_grad = cap_grad + cap_recv[k].astype(f32)
@@ -249,11 +269,10 @@
     cap_dot = jnp.sum(cap_unit * cap_grad, axis=1, keepdims=True)
     cap_grad_ref[...] = (cap_grad - cap_unit * cap_dot) * cap_inv
 
-    for copy in raw_copies:
-        copy.wait_recv()
-    clip_grad_ref[...] = lax.dot_general(
-        raw_all[...].reshape(rows, width), proj_v[...], (((1,), (1,)), ((), ())), preferred_element_type=f32
-    )
+    for k in range(1, tensor):
+        for q in range(nq):
+            raw_copies[q * (tensor - 1) + k - 1].wait_recv()
+        clip_rows(lax.rem(t + (tensor - k), tensor))
     for copy in started:
         copy.wait_send()
 
@@ -287,6 +306,7 @@
     nb = inner * tensor
     vrow = rows // tensor
     tile_rows = nb * vrow
+    nq = chunks(vrow)
     vmem = pl.BlockSpec(memory_space=pltpu.VMEM)
     hbm = pl.BlockSpec(memory_space=pltpu.HBM)
     dma = pltpu.SemaphoreType.DMA
@@ -298,7 +318,7 @@
             jax.ShapeDtypeStruct((ccol, width), f32),
             jax.ShapeDtypeStruct((1, rows), f32),
         ),
-        in_specs=[pl.BlockSpec(memory_space=pltpu.SMEM), hbm, hbm, hbm, hbm],
+        in_specs=[pl.BlockSpec(memory_space=pltpu.SMEM)] + [hbm] * 4,
         out_specs=(vmem, vmem, vmem),
         scratch_shapes=[
             pltpu.VMEM((1, pair_perm.shape[0]), jnp.int32),
@@ -321,19 +341,25 @@
             pltpu.VMEM((no, ccol, width), bf16),
             pltpu.VMEM((tensor, vrow, width), bf16),
             dma((4,)),
-            *[dma((nt,))] * 2,
+            *[dma((nt, nq))] * 2,
             *[dma((no,))] * 2,
             *[dma((outer,))] * 2,
+            *[dma((nr, nq))] * 2,
             *[dma((nr,))] * 2,
-            *[dma((nr,))] * 2,
-            *[dma((nr,))] * 2,
+            *[dma((nr, nq))] * 2,
             *[dma((outer,))] * 2,
             *[dma((no,))] * 2,
-            *[dma((nt,))] * 2,
+            *[dma((nt, nq))] * 2,
         ],
         compiler_params=pltpu.CompilerParams(collective_id=0, has_side_effects=True, vmem_limit_bytes=48 * 1024 * 1024),
         name="contrastive_step",
-    )(logit_scale, *[pltpu.with_memory_space_constraint(x, pltpu.HBM) for x in (pair_perm.reshape(1, -1), clip_feats, proj_weight, caption_emb)])
+    )(
+        logit_scale,
+        *[
+            pltpu.with_memory_space_constraint(x, pltpu.HBM)
+            for x in (pair_perm.reshape(1, -1), clip_feats, proj_weight, caption_emb)
+        ]
+    )
     clip_grad, caption_grad, losses = store_results(clip_grad, caption_grad, losses)
     return clip_grad, caption_grad, losses.reshape(rows)
 

time: 30.7 us -> 30 us (0.977)
  Pallas kernels: 29.2 us -> 28.5 us
    pallas_call x1, Pallas kernels: 28.4 us -> 27.7 us  [body(): pl.pallas_call(functools.partial(kernel, dp, tensor), out_shape=(jax.Shap...]
where the time goes in v4:
time: 30 us; the launch traced here: 29.8 us
  Pallas kernels  28.5 us (95%)
  between operations  1.29 us (4%)
    pallas_call x1, Pallas kernels, body(): pl.pallas_call(functools.partial(kernel, dp, tensor), out_shape=(jax.Shap...  27.7 us
    pallas_call x1, Pallas kernels, store_results(): pl.pallas_call(store_kernel, out_shape=tuple((jax.ShapeDtypeStruct(v.shap...  0.79 us

profile of v4, /device:TPU:0, one launch (start us, length us, event | category | flops | bytes accessed | tf_op | source)
XLA Modules:
  0.0 29.8 jit_solution(17251438909648480311)
XLA Ops:
  1.3 27.7 %contrastive_step.1 = (f32[128,640]{1,0:T(8,128)S(1)}, f32[64,512]{1,0:T(8,128)S(1)}, f32[1,128]{1,0:T(1,128)S(1)}) custom-call(f32[1]{0:T(128)S(6)} %copy.8.logit_ref, s32[1,2048]{1,0:T(1,128)} %bitcast.2, bf16[128,640]{1,0:T(8,128)(2,1)} %clip_hbm.1, bf16[640,512]{1,0:T(8,128)(2,1)} %proj_hbm.1, bf16[64,512]{1,0:T(8,128)(2,1)} %cap_hbm.1), custom_call_target="tpu_custom_call" | custom-call | tf_op jit(solution)/shard_map/contrastive_step/pallas_call | solution.py:314
  29.0 0.8 %store_results.1 = (f32[128,640]{1,0:T(8,128)}, f32[64,512]{1,0:T(8,128)}, f32[1,128]{1,0:T(1,128)}) custom-call(f32[128,640]{1,0:T(8,128)S(1)} %get-tuple-element.9.refs_0_, f32[64,512]{1,0:T(8,128)S(1)} %get-tuple-element.10.refs_1_, f32[1,128]{1,0:T(1,128)S(1)} %get-tuple-element.11.refs_2_), custom_call_target="tpu_custom_call" | custom-call | tf_op jit(solution)/shard_map/store_results/pallas_call | solution.py:291
